TPU v7x, 256 devices: a whole 4x4x8 slice. The times are simulated.
256 devices in a mesh: leaf: 16 (over y, x), col: 16 (over z, core).
Axes of the slice: x: 4, y: 4, z: 8, core: 2. Of those that a mesh axis runs over, the one named last changes fastest.
Arguments:
- right_sides: bfloat16 [16, 2, 1792, 128], P('leaf', None, 'col'), may hold values from -6 to 6
- leaf_inverse: bfloat16 [16, 1792, 1792], P('leaf', 'col'), as said below
- upper_inverse: bfloat16 [16, 1792, 1792], P('leaf', 'col'), as said below
- leaf_update: bfloat16 [16, 4, 1792, 512], P('leaf', None, 'col'), may hold values from -0.0625 to 0.0625
- upper_update: bfloat16 [16, 4, 1792, 512], P('leaf', None, 'col'), may hold values from -0.0625 to 0.0625
- live_rows: int32 [16, 2], P('leaf'), may hold values from 896 to 1792, as said below
- tile_map: int32 [16, 2, 4, 512], P('leaf'), may hold values from 0 to 1791, as said below
Outputs:
- solution: bfloat16 [16, 2, 1792, 128], P('leaf', None, 'col')
Inputs may be any that keep to these rules, and one draw needn't show every extreme that they name: `leaf_inverse`: zero above the diagonal, nonzero on it. `upper_inverse`: zero above the diagonal, nonzero on it. `live_rows`: one supernode has all 1792 rows live and one has 896. `tile_map`: the rows of one tile are distinct and increasing.
All inputs are finite; a program needn't handle non-finite values.
Results may differ from a plain program's by a relative error of at most 0.0075.
Values may be sent and summed in bfloat16 or wider, within the bound.
No kernel may reach another device: no remote copies, remote signals or barrier semaphores. Data moves between devices by JAX's collectives and lax.ppermute only.
A program may use at most 64 MiB of HBM per device.

v0:
```python
import jax
import jax.numpy as jnp
from jax import lax
from jax.sharding import PartitionSpec as P

BF = jnp.bfloat16
F32 = jnp.float32


def dot(a, b, ca, cb):
    return lax.dot_general(a, b, (((ca,), (cb,)), ((), ())), preferred_element_type=F32)


def split_dot(a, b, ca, cb):
    hi = a.astype(BF)
    lo = (a - hi.astype(F32)).astype(BF)
    n = a.shape[0]
    both = dot(jnp.concatenate([hi, lo], axis=0), b, ca, cb)
    return both[:n] + both[n:]


def shards(
    right_sides, leaf_inverse, upper_inverse, leaf_update, upper_update, live_rows, tile_map
):
    leaf_count = lax.axis_size("leaf")
    col_count = lax.axis_size("col")
    depth = leaf_count.bit_length() - 1
    rows_dev = leaf_inverse.shape[1]
    rows = leaf_inverse.shape[2]
    width = right_sides.shape[3]
    part = width // col_count
    tile_len = tile_map.shape[3]
    leaf_id = lax.axis_index("leaf")
    col_id = lax.axis_index("col")
    all_rows = lax.broadcasted_iota(jnp.int32, (1, rows), 1)
    mask_up = (all_rows < live_rows[0, 1]).astype(F32)
    rows_full = lax.broadcasted_iota(jnp.int32, (rows, 1), 0)
    own_rows = col_id * rows_dev + lax.broadcasted_iota(jnp.int32, (rows_dev, 1), 0)
    mask_leaf = (own_rows < live_rows[0, 0]).astype(F32)
    node_level = jnp.zeros((), jnp.int32)
    for height in range(1, depth + 1):
        node_level = node_level + ((leaf_id % 2 ** (height - 1) == 0) & (leaf_id > 0)).astype(
            jnp.int32
        )
    inv_up = lax.all_gather(upper_inverse[0], "col", axis=0, tiled=True)
    upd_up = lax.all_gather(upper_update[0, : depth - 1], "col", axis=1, tiled=True)
    picks = (
        tile_map[0][:, :, :, None] == lax.broadcasted_iota(jnp.int32, (1, 1, 1, rows), 3)
    ).astype(BF)
    pick_leaf, pick_up = (picks[0], picks[1])
    both = lax.all_gather(right_sides[0], "col", axis=1, tiled=True)
    r_leaf = jnp.where(rows_full < live_rows[0, 0], both[0], jnp.zeros_like(both[0]))
    base_up = lax.dynamic_slice_in_dim(both[1].T, col_id * part, part, 0).astype(F32)
    y_leaf = (dot(leaf_inverse[0], r_leaf, 1, 0) * mask_leaf).astype(BF)
    terms = jnp.concatenate(
        [dot(y_leaf, leaf_update[0, s], 0, 0) for s in range(depth)], axis=1
    ).astype(BF)
    swapped = lax.all_to_all(
        terms.reshape(col_count, part, depth * tile_len), "col", 0, 0, tiled=False
    )
    z_leaf = jnp.sum(swapped.astype(F32), axis=0)
    acc = jnp.stack(
        [
            split_dot(z_leaf[:, s * tile_len : (s + 1) * tile_len], pick_leaf[s], 1, 0)
            for s in range(depth)
        ]
    )
    nodes = range(1, leaf_count)

    def level_of(node):
        return (node & -node).bit_length()

    y_up = jnp.zeros((part, rows), BF)
    for height in range(1, depth + 1):
        if height == 1:
            got = lax.ppermute(acc, "leaf", [(i, i + 1) for i in range(0, leaf_count, 2)])
            acc = jnp.where(leaf_id % 2 == 1, acc + got, 0.0)
        else:
            step = 2 ** (height - 2)
            ups = [i for i in nodes if level_of(i) == height]
            acc = lax.ppermute(acc, "leaf", [(i - step, i) for i in ups]) + lax.ppermute(
                acc, "leaf", [(i + step, i) for i in ups]
            )
        r = ((base_up - acc[0]) * mask_up).astype(BF)
        y = (dot(r, inv_up, 1, 1) * mask_up).astype(BF)
        y_up = jnp.where(node_level == height, y, y_up)
        acc = acc[1:]
        if height < depth:
            acc = acc + jnp.stack(
                [
                    split_dot(dot(y, upd_up[s], 1, 0), pick_up[s], 1, 0)
                    for s in range(depth - height)
                ]
            )
    x_up = jnp.zeros((part, rows), BF)
    above = None
    for height in range(depth, 0, -1):
        if height == depth:
            pulled = jnp.zeros((part, rows), F32)
        else:
            pulled = sum(
                (
                    dot(dot(above[s], pick_up[s], 1, 1).astype(BF), upd_up[s], 1, 1)
                    for s in range(depth - height)
                )
            )
        v = ((y_up.astype(F32) - pulled) * mask_up).astype(BF)
        x = (dot(v, inv_up, 1, 0) * mask_up).astype(BF)
        x_up = jnp.where(node_level == height, x, x_up)
        above = x[None] if above is None else jnp.concatenate([x[None], above])
        if height == 1:
            got = lax.ppermute(above, "leaf", [(i + 1, i) for i in range(0, leaf_count, 2)])
            above = jnp.where(leaf_id % 2 == 1, above, got)
        else:
            step = 2 ** (height - 2)
            ups = [i for i in nodes if level_of(i) == height]
            above = lax.ppermute(above, "leaf", [(i, i - step) for i in ups]) + lax.ppermute(
                above, "leaf", [(i, i + step) for i in ups]
            )
    tiles = jnp.concatenate(
        [dot(above[s], pick_leaf[s], 1, 1).astype(BF) for s in range(depth)], axis=1
    )
    tiles = lax.all_gather(tiles, "col", axis=0, tiled=True)
    pulled = sum(
        (
            dot(leaf_update[0, s], tiles[:, s * tile_len : (s + 1) * tile_len], 1, 1)
            for s in range(depth)
        )
    )
    v = ((y_leaf.astype(F32) - pulled) * mask_leaf).astype(BF)
    terms = dot(leaf_inverse[0], v, 0, 0).astype(BF).reshape(col_count, rows_dev, width)
    swapped = lax.all_to_all(terms, "col", 0, 0, tiled=False)
    x_leaf = (jnp.sum(swapped.astype(F32), axis=0) * mask_leaf).astype(BF)
    x_up = jnp.where(leaf_id > 0, x_up, jnp.zeros_like(x_up))
    up_rows = lax.all_to_all(
        x_up.reshape(part, col_count, rows_dev).transpose(1, 0, 2), "col", 0, 0, tiled=False
    )
    up_rows = up_rows.reshape(width, rows_dev).T
    return jnp.stack([x_leaf, up_rows])[None]


def solution(mesh):
    placed = (
        P("leaf", None, "col", None),
        P("leaf", "col", None),
        P("leaf", "col", None),
        P("leaf", None, "col", None),
        P("leaf", None, "col", None),
        P("leaf", None),
        P("leaf", None, None, None),
    )
    return jax.shard_map(
        shards, mesh=mesh, in_specs=placed, out_specs=P("leaf", None, "col", None), check_vma=False
    )
```

profile of v0, /device:TPU:23, one launch (start us, length us, event | category | flops | bytes accessed | tf_op | source)
XLA Modules:
  0.0 273.4 jit_solution(10136190612062378976)
XLA Ops:
  6.5 0.7 all-gather.6.cloned.1.call-update
  7.3 1.7 slice.255
  9.1 0.9 copy.25
  10.0 1.3 fusion.229
  12.5 25.3 %all-gather = bf16[1,2,1792,128]{3,1,0,2:T(2,128)(2,1)S(1)} all-gather(bf16[1,2,112,128]{3,1,0,2:T(2,128)(2,1)S(1)} %copy.25), channel_id=2, replica_groups=mesh['leaf'=16,'col'=16] {'col'}, dimensions={2}, use_global_device_ids=true | all-gather | bytes 974848 | tf_op jit(solution)/shard_map/all_gather | solution.py:51
  37.9 1.3 fusion.228
  41.2 0.9 pad_maximum_fusion
  42.0 4.2 %all-to-all-start = ((bf16[16,8,2048]{2,1,0:T(8,128)(2,1)}), bf16[16,8,2048]{2,1,0:T(8,128)(2,1)S(1)}, u32[]{:S(2)}, u32[]{:S(2)}) async-start(bf16[16,8,2048]{2,1,0:T(8,128)(2,1)} %pad_maximum_fusion), calls=%async_computation | async-start | bytes 1048576 | tf_op jit(solution)/shard_map/all_to_all | solution.py:58
  46.2 6.7 %iota_compare_fusion = pred[2,4,512,1792]{3,2,1,0:T(32,128)(4,1)} fusion(s32[2,4,512]{2,1,0:T(4,128)S(1)} %bitcast.352), kind=kLoop, calls=%fused_computation | loop fusion | flops 7340032 | bytes 7356416 | tf_op jit(solution)/shard_map/eq | solution.py:48
  52.9 1.6 slice_bitcast_fusion.2
  54.5 14.0 %all-to-all-done = bf16[16,8,2048]{2,1,0:T(8,128)(2,1)S(1)} async-done(((bf16[16,8,2048]{2,1,0:T(8,128)(2,1)}), bf16[16,8,2048]{2,1,0:T(8,128)(2,1)S(1)}, u32[]{:S(2)}, u32[]{:S(2)}) %all-to-all-start) | async-done | bytes 524320 | tf_op jit(solution)/shard_map/all_to_all | solution.py:58
  68.6 1.8 fusion.17
  70.5 1.8 fusion.19
  72.3 1.8 fusion.21
  74.1 1.8 fusion.23
  76.0 0.7 pad_maximum_fusion.1
  76.7 1.3 collective-permute-start
  78.0 1.2 constant_dynamic-slice_fusion
  79.1 0.7 copy.34
  80.5 5.4 %collective-permute-done = f32[4,8,1792]{2,1,0:T(8,128)} collective-permute-done((f32[4,8,1792]{2,1,0:T(8,128)}, f32[4,8,1792]{2,1,0:T(8,128)}, u32[]{:S(2)}, u32[]{:S(2)}) %collective-permute-start) | collective-permute-done | bytes 229408 | tf_op jit(solution)/shard_map/ppermute | solution.py:76
  86.0 1.0 add_select_fusion
  87.6 5.3 %fusion.77 = bf16[8,1792]{1,0:T(8,128)(2,1)} fusion(bf16[1,1792,1792]{2,1,0:T(8,128)(2,1)} %all-gather.6.cloned.1.call-done, f32[4,8,1792]{2,1,0:T(8,128)S(1)} %add_select_fusion, bf16[1,1,1792,8]{2,3,1,0:T(8,128)(2,1)S(1)} %copy.34, f32[1792]{0:T(1024)S(1)} %fusion.216), kind=kOutput, calls=%fused_computation.60 | convolution fusion | flops 51466240 | bytes 6553600 | tf_op jit(solution)/shard_map/dot_general | solution.py:11
  93.0 23.7 %all-gather.8.cloned.1.call-done = bf16[1,3,1792,512]{3,2,1,0:T(8,128)(2,1)} async-done(((bf16[1,3,112,512]{3,2,1,0:T(8,128)(2,1)}), bf16[1,3,1792,512]{3,2,1,0:T(8,128)(2,1)}) %all-gather.8.cloned.1.call-update) | async-done | bytes 5505040 | tf_op jit(solution)/shard_map/all_gather | solution.py:46
  116.6 2.0 subtract_convert_fusion.5
  119.2 1.9 subtract_convert_fusion.4
  121.1 2.0 fusion.104
  123.0 1.1 subtract_convert_fusion.3
  124.1 1.8 fusion.25
  126.0 0.7 collective-permute-start.1
  126.7 3.1 %collective-permute-start.2 = (f32[3,8,1792]{2,1,0:T(8,128)S(1)}, f32[3,8,1792]{2,1,0:T(8,128)S(1)}, u32[]{:S(2)}, u32[]{:S(2)}) collective-permute-start(f32[3,8,1792]{2,1,0:T(8,128)S(1)} %slice_add_fusion), channel_id=1, source_target_pairs={{48,32},{112,96},{176,160},{240,224},{49,33},{113,97},{177,161},{2... | collective-permute-start | bytes 516104 | tf_op jit(solution)/shard_map/ppermute | solution.py:81
  129.8 3.4 %collective-permute-done.2 = f32[3,8,1792]{2,1,0:T(8,128)S(1)} collective-permute-done((f32[3,8,1792]{2,1,0:T(8,128)S(1)}, f32[3,8,1792]{2,1,0:T(8,128)S(1)}, u32[]{:S(2)}, u32[]{:S(2)}) %collective-permute-start.2) | collective-permute-done | bytes 172064 | tf_op jit(solution)/shard_map/ppermute | solution.py:81
  133.3 1.8 fusion.74
  136.3 1.8 fusion.103
  138.2 0.7 collective-permute-start.3
  138.9 0.8 collective-permute-start.4
  139.8 1.8 fusion.71
  142.5 0.7 collective-permute-start.5
  143.2 0.7 collective-permute-start.6
  143.9 4.6 %fusion.86 = f32[8,1792]{1,0:T(8,128)S(1)} fusion(bf16[1,1792,1792]{2,1,0:T(8,128)(2,1)} %all-gather.6.cloned.1.call-done, f32[1,8,1792]{2,1,0:T(8,128)S(1)} %collective-permute-done.5, f32[1,8,1792]{2,1,0:T(8,128)S(1)} %collective-permute-done.6, bf16[1,1,1792,8]{2,3,1,0:T(8,128)(2,1)} %copy-done.6, bf16[8,1792]{1,0:T(8,128)(2,1)} %copy-done.9, ...), kind=kOutput, calls=%fused_computation.65 | convolution fusion | flops 51552256 | bytes 6716420 | tf_op jit(solution)/shard_map/dot_general | solution.py:11
  148.5 3.8 %fusion.65 = bf16[8,1792]{1,0:T(8,128)(2,1)S(1)} fusion(bf16[1,1792,1792]{2,1,0:T(8,128)(2,1)} %all-gather.6.cloned.1.call-done, f32[8,1792]{1,0:T(8,128)S(1)} %fusion.86, f32[1792]{0:T(1024)S(1)} %fusion.216), kind=kOutput, calls=%fused_computation.56 | convolution fusion | flops 51437568 | bytes 6515712 | tf_op jit(solution)/shard_map/dot_general | solution.py:11
  152.3 0.7 collective-permute-start.7
  154.3 4.9 %fusion.62 = bf16[8,1792]{1,0:T(8,128)(2,1)S(1)} fusion(bf16[1,1792,1792]{2,1,0:T(8,128)(2,1)} %all-gather.6.cloned.1.call-done, f32[8,1792]{1,0:T(8,128)S(1)} %fusion.86, bf16[8,512]{1,0:T(8,128)(2,1)S(1)} %convolution_convert_fusion.9, bf16[1,3,1792,512]{3,2,1,0:T(8,128)(2,1)} %all-gather.8.cloned.1.call-done, f32[1792]{0:T(1024)S(1)} %fusion.216), kind=kOutput, calls=%fused_computation.55 | convolution fusion | flops 66131968 | bytes 8368128 | tf_op jit(solution)/shard_map/dot_general | solution.py:11
  159.3 0.7 collective-permute-start.10
  159.9 0.7 collective-permute-start.9
  160.6 2.7 fusion.101
  163.3 3.1 %fusion.81 = bf16[8,1792]{1,0:T(8,128)(2,1)S(1)} fusion(f32[8,1792]{1,0:T(8,128)S(1)} %fusion.86, f32[8,1792]{1,0:T(8,128)S(1)} %fusion.101, bf16[1,3,1792,512]{3,2,1,0:T(8,128)(2,1)} %all-gather.8.cloned.1.call-done, pred[2,4,512,1792]{3,2,1,0:T(32,128)(4,1)} %iota_compare_fusion, bf16[2,8,1792]{2,1,0:T(8,128)(2,1)S(1)} %add.144, f32[1792]{0:T(1024)S(1)} %fusion.216), kind=kOutput, calls=%fused_computation.62 | convolution fusion | flops 29421568 | bytes 2932736 | tf_op jit(solution)/shard_map/dot_general | solution.py:11
  166.4 3.8 %fusion.59 = bf16[8,1792]{1,0:T(8,128)(2,1)S(1)} fusion(bf16[8,1792]{1,0:T(8,128)(2,1)S(1)} %fusion.81, bf16[1,1792,1792]{2,1,0:T(8,128)(2,1)} %all-gather.6.cloned.1.call-done, f32[1792]{0:T(1024)S(1)} %fusion.216), kind=kOutput, calls=%fused_computation.54 | convolution fusion | flops 51408896 | bytes 6487040 | tf_op jit(solution)/shard_map/dot_general | solution.py:11
  170.2 0.7 collective-permute-start.11
  170.9 1.3 collective-permute-start.12
  172.2 20.2 %collective-permute-done.12 = bf16[3,8,1792]{2,1,0:T(8,128)(2,1)S(1)} collective-permute-done((bf16[3,8,1792]{2,1,0:T(8,128)(2,1)S(1)}, bf16[3,8,1792]{2,1,0:T(8,128)(2,1)S(1)}, u32[]{:S(2)}, u32[]{:S(2)}) %collective-permute-start.12) | collective-permute-done | bytes 86048 | tf_op jit(solution)/shard_map/ppermute | solution.py:117
  192.5 2.7 fusion.102
  195.1 3.1 %convolution_add_fusion.1 = f32[8,1792]{1,0:T(8,128)S(1)} fusion(f32[8,1792]{1,0:T(8,128)S(1)} %fusion.102, bf16[1,3,1792,512]{3,2,1,0:T(8,128)(2,1)} %all-gather.8.cloned.1.call-done, pred[2,4,512,1792]{3,2,1,0:T(32,128)(4,1)} %iota_compare_fusion, bf16[3,8,1792]{2,1,0:T(8,128)(2,1)S(1)} %add.146), kind=kOutput, calls=%fused_computation.39 | convolution fusion | flops 29378560 | bytes 2895872 | tf_op jit(solution)/shard_map/dot_general | solution.py:11
  198.2 3.1 %fusion.82 = bf16[8,1792]{1,0:T(8,128)(2,1)S(1)} fusion(f32[8,1792]{1,0:T(8,128)S(1)} %fusion.86, f32[8,1792]{1,0:T(8,128)S(1)} %convolution_add_fusion.1, bf16[1,3,1792,512]{3,2,1,0:T(8,128)(2,1)} %all-gather.8.cloned.1.call-done, pred[2,4,512,1792]{3,2,1,0:T(32,128)(4,1)} %iota_compare_fusion, bf16[3,8,1792]{2,1,0:T(8,128)(2,1)S(1)} %add.146, ...), kind=kOutput, calls=%fused_computation.63 | convolution fusion | flops 29421568 | bytes 2932736 | tf_op jit(solution)/shard_map/dot_general | solution.py:11
  201.4 3.8 %select_select_fusion = (bf16[8,1792]{1,0:T(8,128)(2,1)S(1)}, bf16[8,1792]{1,0:T(8,128)(2,1)S(1)}) fusion(bf16[8,1792]{1,0:T(8,128)(2,1)S(1)} %fusion.59, bf16[8,1792]{1,0:T(8,128)(2,1)S(1)} %fusion.62, bf16[8,1792]{1,0:T(8,128)(2,1)S(1)} %fusion.65, pred[]{:T(512)S(6)} %gt.2, pred[]{:T(512)S(6)} %eq.63, pred[]{:T(512)S(6)} %eq.62, pred[]{:T(512)S(6)} %eq.61, ...), kind=kOutput, calls=%fused_computation.202 | convolution fusion | flops 51480576 | bytes 6601733 | tf_op jit(solution)/shard_map/dot_general | solution.py:11
  205.2 1.7 collective-permute-start.13
  207.6 9.4 %all-to-all-start.2 = ((bf16[16,8,112]{2,1,0:T(8,128)(2,1)}), bf16[16,8,112]{2,1,0:T(8,128)(2,1)S(1)}, u32[]{:S(2)}, u32[]{:S(2)}) async-start(bf16[16,8,112]{2,1,0:T(8,128)(2,1)} %bitcast.341), calls=%async_computation.2 | async-start | bytes 65536 | tf_op jit(solution)/shard_map/all_to_all | solution.py:135
  217.0 1.9 fusion.100
  218.9 1.9 fusion.99
  220.8 1.9 fusion.98
  222.6 1.9 fusion.97
  224.5 18.6 %all_gather.15 = bf16[128,2048]{1,0:T(8,128)(2,1)S(1)} all-gather(bf16[8,2048]{1,0:T(8,128)(2,1)S(1)} %pad_maximum_fusion.5), channel_id=1, replica_groups=mesh['leaf'=16,'col'=16] {'col'}, dimensions={0}, use_global_device_ids=true | all-gather | bytes 557056 | tf_op jit(solution)/shard_map/all_gather | solution.py:123
  244.2 1.0 copy.29
  245.2 4.7 %all-to-all-start.1 = ((bf16[16,112,128]{2,1,0:T(8,128)(2,1)}), bf16[16,112,128]{2,1,0:T(8,128)(2,1)S(1)}, u32[]{:S(2)}, u32[]{:S(2)}) async-start(bf16[16,112,128]{2,1,0:T(8,128)(2,1)} %bitcast.58), calls=%async_computation.1 | async-start | bytes 917504 | tf_op jit(solution)/shard_map/all_to_all | solution.py:132
  250.0 15.7 %all-to-all-done.1 = bf16[16,112,128]{2,1,0:T(8,128)(2,1)S(1)} async-done(((bf16[16,112,128]{2,1,0:T(8,128)(2,1)}), bf16[16,112,128]{2,1,0:T(8,128)(2,1)S(1)}, u32[]{:S(2)}, u32[]{:S(2)}) %all-to-all-start.1) | async-done | bytes 458784 | tf_op jit(solution)/shard_map/all_to_all | solution.py:132
  (100 shorter events, 11.6 us)
Async XLA Ops:
  6.5 32.6 %copy-start = (bf16[1,112,1792]{2,1,0:T(8,128)(2,1)S(1)}, bf16[1,112,1792]{2,1,0:T(8,128)(2,1)}, u32[]{:S(2)}) copy-start(bf16[1,112,1792]{2,1,0:T(8,128)(2,1)} %param.8) | copy-start | bytes 1204228
  6.5 33.9 %copy-start.2 = (bf16[1,4,112,512]{3,2,1,0:T(8,128)(2,1)S(1)}, bf16[1,4,112,512]{3,2,1,0:T(8,128)(2,1)}, u32[]{:S(2)}) copy-start(bf16[1,4,112,512]{3,2,1,0:T(8,128)(2,1)} %param.10) | copy-start | bytes 1376260
  6.5 39.7 %copy-start.12 = (s32[1,2,4,512]{3,2,1,0:T(4,128)S(1)}, s32[1,2,4,512]{3,2,1,0:T(4,128)}, u32[]{:S(2)}) copy-start(s32[1,2,4,512]{3,2,1,0:T(4,128)} %param.13) | copy-start | bytes 49156
  6.5 80.4 %all-gather.6.cloned.1.call-start = ((), (), s32[]{:S(2)}) async-start(), calls=%async_computation.3 | async-start | bytes 6823936 | tf_op jit(solution)/shard_map/all_gather | solution.py:45
  7.3 109.4 %all-gather.8.cloned.1.call-start = ((), (), s32[]{:S(2)}) async-start(), calls=%async_computation.4 | async-start | bytes 5849088 | tf_op jit(solution)/shard_map/all_gather | solution.py:46
  11.9 41.0 %copy-start.13 = (f32[112]{0:T(128)}, f32[112]{0:T(128)S(1)}, u32[]{:S(2)}) copy-start(f32[112]{0:T(128)S(1)} %compare_convert_fusion) | copy-start | bytes 1348
  39.7 0.6 copy-start.10
  42.0 26.5 %all-to-all-start = ((bf16[16,8,2048]{2,1,0:T(8,128)(2,1)}), bf16[16,8,2048]{2,1,0:T(8,128)(2,1)S(1)}, u32[]{:S(2)}, u32[]{:S(2)}) async-start(bf16[16,8,2048]{2,1,0:T(8,128)(2,1)} %pad_maximum_fusion), calls=%async_computation | async-start | bytes 1048576 | tf_op jit(solution)/shard_map/all_to_all | solution.py:58
  76.7 9.3 %collective-permute-start = (f32[4,8,1792]{2,1,0:T(8,128)}, f32[4,8,1792]{2,1,0:T(8,128)}, u32[]{:S(2)}, u32[]{:S(2)}) collective-permute-start(f32[4,8,1792]{2,1,0:T(8,128)} %pad_maximum_fusion.1), channel_id=1, source_target_pairs={{0,16},{32,48},{64,80},{96,112},{128,144},{160,176},{192,208},{224... | collective-permute-start | bytes 688136 | tf_op jit(solution)/shard_map/ppermute | solution.py:76
  79.9 7.1 %copy-start.6 = (bf16[1,1,1792,8]{2,3,1,0:T(8,128)(2,1)}, bf16[1,1,1792,8]{2,3,1,0:T(8,128)(2,1)S(1)}, u32[]{:S(2)}) copy-start(bf16[1,1,1792,8]{2,3,1,0:T(8,128)(2,1)S(1)} %copy.34) | copy-start | bytes 86020
  86.9 0.7 copy-start.4
  93.0 40.3 %slice-start = ((s8[6422528]{0:T(1024)(128)(4,1)}), s8[2228224]{0:T(1024)(128)(4,1)S(1)}, s32[]{:S(2)}) async-start(s8[6422528]{0:T(1024)(128)(4,1)} %bitcast.342), calls=%async_computation.5 | async-start | bytes 4456448
  116.6 6.4 %copy-start.1 = (bf16[1,3,1792,512]{3,2,1,0:T(8,128)(2,1)S(1)}, bf16[1,3,1792,512]{3,2,1,0:T(8,128)(2,1)}, u32[]{:S(2)}) copy-start(bf16[1,3,1792,512]{3,2,1,0:T(8,128)(2,1)} %all-gather.8.cloned.1.call-done) | copy-start | bytes 16515076
  116.6 9.3 %copy-start.5 = (f32[4,8,1792]{2,1,0:T(8,128)S(1)}, f32[4,8,1792]{2,1,0:T(8,128)}, u32[]{:S(2)}) copy-start(f32[4,8,1792]{2,1,0:T(8,128)} %copy-done.4) | copy-start | bytes 688132
  116.6 16.6 %copy-start.7 = (bf16[1,1,1792,8]{2,3,1,0:T(8,128)(2,1)S(1)}, bf16[1,1,1792,8]{2,3,1,0:T(8,128)(2,1)}, u32[]{:S(2)}) copy-start(bf16[1,1,1792,8]{2,3,1,0:T(8,128)(2,1)} %copy-done.6) | copy-start | bytes 86020
  121.1 12.2 %slice-start.1 = ((s8[6422528]{0:T(1024)(128)(4,1)}), s8[4194304]{0:T(1024)(128)(4,1)S(1)}, s32[]{:S(2)}) async-start(s8[6422528]{0:T(1024)(128)(4,1)} %bitcast.342), calls=%async_computation.6 | async-start | bytes 8388608
  126.0 3.8 %collective-permute-start.1 = (f32[3,8,1792]{2,1,0:T(8,128)S(1)}, f32[3,8,1792]{2,1,0:T(8,128)S(1)}, u32[]{:S(2)}, u32[]{:S(2)}) collective-permute-start(f32[3,8,1792]{2,1,0:T(8,128)S(1)} %slice_add_fusion), channel_id=1, source_target_pairs={{16,32},{80,96},{144,160},{208,224},{17,33},{81,97},{145,161},{209... | collective-permute-start | bytes 516104 | tf_op jit(solution)/shard_map/ppermute | solution.py:81
  126.7 6.5 %collective-permute-start.2 = (f32[3,8,1792]{2,1,0:T(8,128)S(1)}, f32[3,8,1792]{2,1,0:T(8,128)S(1)}, u32[]{:S(2)}, u32[]{:S(2)}) collective-permute-start(f32[3,8,1792]{2,1,0:T(8,128)S(1)} %slice_add_fusion), channel_id=1, source_target_pairs={{48,32},{112,96},{176,160},{240,224},{49,33},{113,97},{177,161},{2... | collective-permute-start | bytes 516104 | tf_op jit(solution)/shard_map/ppermute | solution.py:81
  135.1 6.5 %copy-start.8 = (bf16[8,1792]{1,0:T(8,128)(2,1)}, bf16[8,1792]{1,0:T(8,128)(2,1)S(1)}, u32[]{:S(2)}) copy-start(bf16[8,1792]{1,0:T(8,128)(2,1)S(1)} %fusion.74) | copy-start | bytes 86020
  138.2 1.5 collective-permute-start.3
  138.9 0.9 collective-permute-start.4
  141.5 0.9 copy-start.9
  142.5 1.4 collective-permute-start.5
  143.2 0.7 collective-permute-start.6
  152.3 1.3 collective-permute-start.7
  153.0 0.7 collective-permute-start.8
  159.3 1.3 collective-permute-start.10
  159.9 0.7 collective-permute-start.9
  170.2 2.0 collective-permute-start.11
  170.9 21.5 %collective-permute-start.12 = (bf16[3,8,1792]{2,1,0:T(8,128)(2,1)S(1)}, bf16[3,8,1792]{2,1,0:T(8,128)(2,1)S(1)}, u32[]{:S(2)}, u32[]{:S(2)}) collective-permute-start(bf16[3,8,1792]{2,1,0:T(8,128)(2,1)S(1)} %pad_maximum_fusion.3), channel_id=1, source_target_pairs={{32,48},{96,112},{160,176},{224,240},{33,49},{97,113},{161,177},{2... | collective-permute-start | bytes 258056 | tf_op jit(solution)/shard_map/ppermute | solution.py:117
  205.1 38.0 %copy-start.3 = (bf16[1,4,112,512]{3,2,1,0:T(8,128)(2,1)S(1)}, bf16[1,4,112,512]{3,2,1,0:T(8,128)(2,1)}, u32[]{:S(2)}) copy-start(bf16[1,4,112,512]{3,2,1,0:T(8,128)(2,1)} %param.10) | copy-start | bytes 1376260
  205.2 11.8 %collective-permute-start.13 = (bf16[4,8,1792]{2,1,0:T(8,128)(2,1)S(1)}, bf16[4,8,1792]{2,1,0:T(8,128)(2,1)S(1)}, u32[]{:S(2)}, u32[]{:S(2)}) collective-permute-start(bf16[4,8,1792]{2,1,0:T(8,128)(2,1)S(1)} %pad_maximum_fusion.2), channel_id=1, source_target_pairs={{16,0},{48,32},{80,64},{112,96},{144,128},{176,160},{208,192},{240... | collective-permute-start | bytes 344072 | tf_op jit(solution)/shard_map/ppermute | solution.py:112
  207.0 36.7 %copy-start.11 = (bf16[128,112]{0,1:T(8,128)(2,1)S(1)}, bf16[128,112]{0,1:T(8,128)(2,1)}, u32[]{:S(2)}) copy-start(bf16[128,112]{0,1:T(8,128)(2,1)} %copy-done.10) | copy-start | bytes 86020
  207.0 36.7 %copy-start.14 = (f32[112]{0:T(128)S(1)}, f32[112]{0:T(128)}, u32[]{:S(2)}) copy-start(f32[112]{0:T(128)} %copy-done.13) | copy-start | bytes 1348
  207.6 37.6 %all-to-all-start.2 = ((bf16[16,8,112]{2,1,0:T(8,128)(2,1)}), bf16[16,8,112]{2,1,0:T(8,128)(2,1)S(1)}, u32[]{:S(2)}, u32[]{:S(2)}) async-start(bf16[16,8,112]{2,1,0:T(8,128)(2,1)} %bitcast.341), calls=%async_computation.2 | async-start | bytes 65536 | tf_op jit(solution)/shard_map/all_to_all | solution.py:135
  245.2 20.6 %all-to-all-start.1 = ((bf16[16,112,128]{2,1,0:T(8,128)(2,1)}), bf16[16,112,128]{2,1,0:T(8,128)(2,1)S(1)}, u32[]{:S(2)}, u32[]{:S(2)}) async-start(bf16[16,112,128]{2,1,0:T(8,128)(2,1)} %bitcast.58), calls=%async_computation.1 | async-start | bytes 917504 | tf_op jit(solution)/shard_map/all_to_all | solution.py:132
Sparse Core Ops, SparseCore 0:
  9.2 63.2 all-gather.5
  74.3 42.2 all-gather.7
where the time goes:
time: 275 us; the launch traced here: 273 us
  waiting for transfers between devices  83.3 us (30%)
  matrix products  75.3 us (27%)
  blocking collectives  44 us (16%)
  starting transfers between devices  32.5 us (12%)
  between operations  14.1 us (5%)
  other arithmetic  12.3 us (4%)
  local copies, waits for them, and re-layouts  12 us (4%)
    dot_general x43, matrix products, dot(): lax.dot_general(a, b, (((ca,), (cb,)), ((), ())), preferred_element_type=...  75.3 us
    all_gather x1, blocking collectives, shards(): both = lax.all_gather(right_sides[0], 'col', axis=1, tiled=True)  25.3 us
    all_gather x1, waiting for transfers between devices, shards(): lax.all_gather(upper_update[0, :depth - 1], 'col', axis=1, tiled=True)  23.7 us
    ppermute x3, waiting for transfers between devices, shards(): lax.ppermute(above, 'leaf', [(i, i + step) for i in ups])  20.2 us
    all_gather x1, blocking collectives, shards(): tiles = lax.all_gather(tiles, 'col', axis=0, tiled=True)  18.6 us
    all_to_all x1, waiting for transfers between devices, shards(): swapped = lax.all_to_all(terms, 'col', 0, 0, tiled=False)  15.7 us
    all_to_all x1, waiting for transfers between devices, shards(): lax.all_to_all(terms.reshape(col_count, part, depth * tile_len), 'col', 0...  14 us
    all_to_all x1, starting transfers between devices, shards(): lax.all_to_all(x_up.reshape(part, col_count, rows_dev).transpose(1, 0, 2)...  9.38 us
  transfers between devices with their start and end apart: 19, of which 6 were waited for; matrix products, arithmetic and copies ran while one was open for 16% of the time, Pallas kernels for 0%

commit v1 on v0

--- a/solution.py
+++ b/solution.py
@@ -48,7 +48,9 @@
         tile_map[0][:, :, :, None] == lax.broadcasted_iota(jnp.int32, (1, 1, 1, rows), 3)
     ).astype(BF)
     pick_leaf, pick_up = (picks[0], picks[1])
-    both = lax.all_gather(right_sides[0], "col", axis=1, tiled=True)
+    both = jnp.concatenate(
+        lax.all_to_all(jnp.stack([right_sides[0]] * lax.axis_size("col")), "col", 0, 0), axis=1
+    )
     r_leaf = jnp.where(rows_full < live_rows[0, 0], both[0], jnp.zeros_like(both[0]))
     base_up = lax.dynamic_slice_in_dim(both[1].T, col_id * part, part, 0).astype(F32)
     y_leaf = (dot(leaf_inverse[0], r_leaf, 1, 0) * mask_leaf).astype(BF)

time: 275 us -> 290 us (1.055)
  waiting for transfers between devices: 83.3 us -> 117 us
  blocking collectives: 44 us -> 18.6 us
  starting transfers between devices: 32.5 us -> 42 us
    all_to_all x0 -> x1, waiting for transfers between devices: none -> 30.8 us  [shards(): lax.all_to_all(jnp.stack([right_sides[0]] * lax.axis_size('col')), 'col',...]
    all_gather x1 -> x0, blocking collectives: 25.3 us -> none  [shards(): both = lax.all_gather(right_sides[0], 'col', axis=1, tiled=True)]
    all_to_all x0 -> x1, starting transfers between devices: none -> 9.15 us  [shards(): lax.all_to_all(jnp.stack([right_sides[0]] * lax.axis_size('col')), 'col',...]
  transfers between devices with their start and end apart: 19 -> 20, of which waited for: 6 -> 7; matrix products, arithmetic and copies ran while one was open for 16% -> 14% of each run, Pallas kernels for 0% -> 0%
where the time goes in v1:
time: 290 us; the launch traced here: 288 us
  waiting for transfers between devices  117 us (40%)
  matrix products  74.9 us (26%)
  starting transfers between devices  42 us (14%)
  blocking collectives  18.6 us (6%)
  between operations  14.1 us (5%)
  other arithmetic  11.1 us (4%)
  local copies, waits for them, and re-layouts  10.2 us (4%)
    dot_general x43, matrix products, dot(): lax.dot_general(a, b, (((ca,), (cb,)), ((), ())), preferred_element_type=...  74.9 us
    all_to_all x1, waiting for transfers between devices, shards(): lax.all_to_all(jnp.stack([right_sides[0]] * lax.axis_size('col')), 'col',...  30.8 us
    all_gather x1, waiting for transfers between devices, shards(): lax.all_gather(upper_update[0, :depth - 1], 'col', axis=1, tiled=True)  25.5 us
    ppermute x3, waiting for transfers between devices, shards(): lax.ppermute(above, 'leaf', [(i, i + step) for i in ups])  20.2 us
    all_gather x1, blocking collectives, shards(): tiles = lax.all_gather(tiles, 'col', axis=0, tiled=True)  18.6 us
    all_to_all x1, waiting for transfers between devices, shards(): swapped = lax.all_to_all(terms, 'col', 0, 0, tiled=False)  15.7 us
    all_to_all x1, waiting for transfers between devices, shards(): lax.all_to_all(terms.reshape(col_count, part, depth * tile_len), 'col', 0...  13.3 us
    all_to_all x1, starting transfers between devices, shards(): lax.all_to_all(x_up.reshape(part, col_count, rows_dev).transpose(1, 0, 2)...  9.37 us
  transfers between devices with their start and end apart: 20, of which 7 were waited for; matrix products, arithmetic and copies ran while one was open for 14% of the time, Pallas kernels for 0%

profile of v1, /device:TPU:23, one launch (start us, length us, event | category | flops | bytes accessed | tf_op | source)
XLA Modules:
  0.0 288.1 jit_solution(17616946051565890970)
XLA Ops:
  6.5 0.7 all-gather.5.cloned.1.call-update
  7.3 1.7 slice.257
  9.1 1.9 stack.49
  11.0 9.2 %all-to-all-start = ((bf16[16,2,112,128]{3,2,1,0:T(8,128)(2,1)}), bf16[16,2,112,128]{3,2,1,0:T(8,128)(2,1)S(1)}, u32[]{:S(2)}, u32[]{:S(2)}) async-start(bf16[16,2,112,128]{3,2,1,0:T(8,128)(2,1)} %stack.49), calls=%async_computation | async-start | bytes 1835008 | tf_op jit(solution)/shard_map/all_to_all | solution.py:52
  20.1 1.3 fusion.218
  21.4 0.7 compare_convert_fusion
  22.1 0.7 add_compare_fusion
  22.8 30.8 %all-to-all-done = bf16[16,2,112,128]{3,2,1,0:T(8,128)(2,1)S(1)} async-done(((bf16[16,2,112,128]{3,2,1,0:T(8,128)(2,1)}), bf16[16,2,112,128]{3,2,1,0:T(8,128)(2,1)S(1)}, u32[]{:S(2)}, u32[]{:S(2)}) %all-to-all-start) | async-done | bytes 917536 | tf_op jit(solution)/shard_map/all_to_all | solution.py:52
  55.7 0.9 pad_maximum_fusion
  56.6 4.5 %all-to-all-start.1 = ((bf16[16,8,2048]{2,1,0:T(8,128)(2,1)}), bf16[16,8,2048]{2,1,0:T(8,128)(2,1)S(1)}, u32[]{:S(2)}, u32[]{:S(2)}) async-start(bf16[16,8,2048]{2,1,0:T(8,128)(2,1)} %pad_maximum_fusion), calls=%async_computation.1 | async-start | bytes 1048576 | tf_op jit(solution)/shard_map/all_to_all | solution.py:60
  61.1 6.7 %iota_compare_fusion = pred[2,4,512,1792]{3,2,1,0:T(32,128)(4,1)} fusion(s32[2,4,512]{2,1,0:T(4,128)S(1)} %bitcast.330), kind=kLoop, calls=%fused_computation | loop fusion | flops 7340032 | bytes 7356416 | tf_op jit(solution)/shard_map/eq | solution.py:48
  67.8 0.6 fusion.207
  68.4 1.6 slice_bitcast_fusion.2
  70.0 13.3 %all-to-all-done.1 = bf16[16,8,2048]{2,1,0:T(8,128)(2,1)S(1)} async-done(((bf16[16,8,2048]{2,1,0:T(8,128)(2,1)}), bf16[16,8,2048]{2,1,0:T(8,128)(2,1)S(1)}, u32[]{:S(2)}, u32[]{:S(2)}) %all-to-all-start.1) | async-done | bytes 524320 | tf_op jit(solution)/shard_map/all_to_all | solution.py:60
  83.5 1.8 fusion.17
  85.3 1.8 fusion.19
  87.1 1.8 fusion.21
  88.9 1.8 fusion.23
  90.8 1.3 collective-permute-start
  92.5 7.4 %collective-permute-done = f32[4,8,1792]{2,1,0:T(8,128)S(1)} collective-permute-done((f32[4,8,1792]{2,1,0:T(8,128)S(1)}, f32[4,8,1792]{2,1,0:T(8,128)S(1)}, u32[]{:S(2)}, u32[]{:S(2)}) %collective-permute-start) | collective-permute-done | bytes 229408 | tf_op jit(solution)/shard_map/ppermute | solution.py:78
  100.6 5.2 %fusion.77 = bf16[8,1792]{1,0:T(8,128)(2,1)} fusion(bf16[1,1792,1792]{2,1,0:T(8,128)(2,1)} %all-gather.5.cloned.1.call-done, f32[4,8,1792]{2,1,0:T(8,128)S(1)} %add_select_fusion, bf16[1792,8]{0,1:T(8,128)(2,1)S(1)} %copy.25, f32[1792]{0:T(1024)S(1)} %fusion.207), kind=kOutput, calls=%fused_computation.60 | convolution fusion | flops 51466240 | bytes 6553600 | tf_op jit(solution)/shard_map/dot_general | solution.py:11
  105.8 25.5 %all-gather.7.cloned.1.call-done = bf16[1,3,1792,512]{3,2,1,0:T(8,128)(2,1)} async-done(((bf16[1,3,112,512]{3,2,1,0:T(8,128)(2,1)}), bf16[1,3,1792,512]{3,2,1,0:T(8,128)(2,1)}) %all-gather.7.cloned.1.call-update) | async-done | bytes 5505040 | tf_op jit(solution)/shard_map/all_gather | solution.py:46
  131.3 2.0 subtract_convert_fusion.5
  133.9 1.9 subtract_convert_fusion.4
  135.8 2.0 fusion.104
  137.8 1.1 subtract_convert_fusion.3
  138.8 1.8 fusion.25
  140.7 0.7 collective-permute-start.1
  141.4 3.1 %collective-permute-start.2 = (f32[3,8,1792]{2,1,0:T(8,128)S(1)}, f32[3,8,1792]{2,1,0:T(8,128)S(1)}, u32[]{:S(2)}, u32[]{:S(2)}) collective-permute-start(f32[3,8,1792]{2,1,0:T(8,128)S(1)} %slice_add_fusion), channel_id=1, source_target_pairs={{48,32},{112,96},{176,160},{240,224},{49,33},{113,97},{177,161},{2... | collective-permute-start | bytes 516104 | tf_op jit(solution)/shard_map/ppermute | solution.py:83
  144.5 3.4 %collective-permute-done.2 = f32[3,8,1792]{2,1,0:T(8,128)S(1)} collective-permute-done((f32[3,8,1792]{2,1,0:T(8,128)S(1)}, f32[3,8,1792]{2,1,0:T(8,128)S(1)}, u32[]{:S(2)}, u32[]{:S(2)}) %collective-permute-start.2) | collective-permute-done | bytes 172064 | tf_op jit(solution)/shard_map/ppermute | solution.py:83
  148.0 1.8 fusion.74
  151.0 1.8 fusion.103
  152.9 0.7 collective-permute-start.3
  153.6 0.7 collective-permute-start.4
  154.3 1.8 fusion.71
  157.0 0.7 collective-permute-start.5
  157.7 0.8 collective-permute-start.6
  158.6 4.6 %fusion.86 = f32[8,1792]{1,0:T(8,128)S(1)} fusion(bf16[1,1792,1792]{2,1,0:T(8,128)(2,1)} %all-gather.5.cloned.1.call-done, bf16[1792,8]{0,1:T(8,128)(2,1)} %copy-done.6, f32[1,8,1792]{2,1,0:T(8,128)S(1)} %collective-permute-done.5, f32[1,8,1792]{2,1,0:T(8,128)S(1)} %collective-permute-done.6, bf16[8,1792]{1,0:T(8,128)(2,1)} %copy-done.9, ...), kind=kOutput, calls=%fused_computation.65 | convolution fusion | flops 51552256 | bytes 6716420 | tf_op jit(solution)/shard_map/dot_general | solution.py:11
  163.2 3.8 %fusion.65 = bf16[8,1792]{1,0:T(8,128)(2,1)S(1)} fusion(bf16[1,1792,1792]{2,1,0:T(8,128)(2,1)} %all-gather.5.cloned.1.call-done, f32[8,1792]{1,0:T(8,128)S(1)} %fusion.86, f32[1792]{0:T(1024)S(1)} %fusion.207), kind=kOutput, calls=%fused_computation.56 | convolution fusion | flops 51437568 | bytes 6515712 | tf_op jit(solution)/shard_map/dot_general | solution.py:11
  167.0 0.7 collective-permute-start.7
  167.7 0.7 collective-permute-start.8
  169.0 4.9 %fusion.62 = bf16[8,1792]{1,0:T(8,128)(2,1)S(1)} fusion(bf16[1,1792,1792]{2,1,0:T(8,128)(2,1)} %all-gather.5.cloned.1.call-done, f32[8,1792]{1,0:T(8,128)S(1)} %fusion.86, bf16[8,512]{1,0:T(8,128)(2,1)S(1)} %convolution_convert_fusion.9, bf16[1,3,1792,512]{3,2,1,0:T(8,128)(2,1)} %all-gather.7.cloned.1.call-done, f32[1792]{0:T(1024)S(1)} %fusion.207), kind=kOutput, calls=%fused_computation.55 | convolution fusion | flops 66131968 | bytes 8368128 | tf_op jit(solution)/shard_map/dot_general | solution.py:11
  174.0 0.7 collective-permute-start.10
  174.6 0.7 collective-permute-start.9
  175.4 2.7 fusion.101
  178.0 3.1 %fusion.81 = bf16[8,1792]{1,0:T(8,128)(2,1)S(1)} fusion(f32[8,1792]{1,0:T(8,128)S(1)} %fusion.86, f32[8,1792]{1,0:T(8,128)S(1)} %fusion.101, bf16[1,3,1792,512]{3,2,1,0:T(8,128)(2,1)} %all-gather.7.cloned.1.call-done, pred[2,4,512,1792]{3,2,1,0:T(32,128)(4,1)} %iota_compare_fusion, bf16[2,8,1792]{2,1,0:T(8,128)(2,1)S(1)} %add.145, f32[1792]{0:T(1024)S(1)} %fusion.207), kind=kOutput, calls=%fused_computation.62 | convolution fusion | flops 29421568 | bytes 2932736 | tf_op jit(solution)/shard_map/dot_general | solution.py:11
  181.1 3.8 %fusion.59 = bf16[8,1792]{1,0:T(8,128)(2,1)S(1)} fusion(bf16[8,1792]{1,0:T(8,128)(2,1)S(1)} %fusion.81, bf16[1,1792,1792]{2,1,0:T(8,128)(2,1)} %all-gather.5.cloned.1.call-done, f32[1792]{0:T(1024)S(1)} %fusion.207), kind=kOutput, calls=%fused_computation.54 | convolution fusion | flops 51408896 | bytes 6487040 | tf_op jit(solution)/shard_map/dot_general | solution.py:11
  184.9 0.7 collective-permute-start.11
  185.6 1.3 collective-permute-start.12
  186.9 20.2 %collective-permute-done.12 = bf16[3,8,1792]{2,1,0:T(8,128)(2,1)S(1)} collective-permute-done((bf16[3,8,1792]{2,1,0:T(8,128)(2,1)S(1)}, bf16[3,8,1792]{2,1,0:T(8,128)(2,1)S(1)}, u32[]{:S(2)}, u32[]{:S(2)}) %collective-permute-start.12) | collective-permute-done | bytes 86048 | tf_op jit(solution)/shard_map/ppermute | solution.py:119
  207.2 2.7 fusion.102
  209.8 3.1 %convolution_add_fusion.1 = f32[8,1792]{1,0:T(8,128)S(1)} fusion(f32[8,1792]{1,0:T(8,128)S(1)} %fusion.102, bf16[1,3,1792,512]{3,2,1,0:T(8,128)(2,1)} %all-gather.7.cloned.1.call-done, pred[2,4,512,1792]{3,2,1,0:T(32,128)(4,1)} %iota_compare_fusion, bf16[3,8,1792]{2,1,0:T(8,128)(2,1)S(1)} %add.147), kind=kOutput, calls=%fused_computation.39 | convolution fusion | flops 29378560 | bytes 2895872 | tf_op jit(solution)/shard_map/dot_general | solution.py:11
  213.0 3.1 %fusion.82 = bf16[8,1792]{1,0:T(8,128)(2,1)S(1)} fusion(f32[8,1792]{1,0:T(8,128)S(1)} %fusion.86, f32[8,1792]{1,0:T(8,128)S(1)} %convolution_add_fusion.1, bf16[1,3,1792,512]{3,2,1,0:T(8,128)(2,1)} %all-gather.7.cloned.1.call-done, pred[2,4,512,1792]{3,2,1,0:T(32,128)(4,1)} %iota_compare_fusion, bf16[3,8,1792]{2,1,0:T(8,128)(2,1)S(1)} %add.147, ...), kind=kOutput, calls=%fused_computation.63 | convolution fusion | flops 29421568 | bytes 2932736 | tf_op jit(solution)/shard_map/dot_general | solution.py:11
  216.1 3.8 %select_select_fusion = (bf16[8,1792]{1,0:T(8,128)(2,1)S(1)}, bf16[8,1792]{1,0:T(8,128)(2,1)S(1)}) fusion(bf16[8,1792]{1,0:T(8,128)(2,1)S(1)} %fusion.59, bf16[8,1792]{1,0:T(8,128)(2,1)S(1)} %fusion.62, bf16[8,1792]{1,0:T(8,128)(2,1)S(1)} %fusion.65, pred[]{:T(512)S(6)} %gt.2, pred[]{:T(512)S(6)} %eq.63, pred[]{:T(512)S(6)} %eq.62, pred[]{:T(512)S(6)} %eq.61, ...), kind=kOutput, calls=%fused_computation.194 | convolution fusion | flops 51480576 | bytes 6601733 | tf_op jit(solution)/shard_map/dot_general | solution.py:11
  219.9 1.7 collective-permute-start.13
  222.3 9.4 %all-to-all-start.3 = ((bf16[16,8,112]{2,1,0:T(8,128)(2,1)}), bf16[16,8,112]{2,1,0:T(8,128)(2,1)S(1)}, u32[]{:S(2)}, u32[]{:S(2)}) async-start(bf16[16,8,112]{2,1,0:T(8,128)(2,1)} %bitcast.315), calls=%async_computation.3 | async-start | bytes 65536 | tf_op jit(solution)/shard_map/all_to_all | solution.py:137
  231.7 1.9 fusion.100
  233.6 1.9 fusion.99
  235.5 1.9 fusion.98
  237.3 1.9 fusion.97
  239.2 18.6 %all_gather.11 = bf16[128,2048]{1,0:T(8,128)(2,1)S(1)} all-gather(bf16[8,2048]{1,0:T(8,128)(2,1)S(1)} %pad_maximum_fusion.5), channel_id=1, replica_groups=mesh['leaf'=16,'col'=16] {'col'}, dimensions={0}, use_global_device_ids=true | all-gather | bytes 557056 | tf_op jit(solution)/shard_map/all_gather | solution.py:125
  258.9 1.0 copy.22
  259.9 4.7 %all-to-all-start.2 = ((bf16[16,112,128]{2,1,0:T(8,128)(2,1)}), bf16[16,112,128]{2,1,0:T(8,128)(2,1)S(1)}, u32[]{:S(2)}, u32[]{:S(2)}) async-start(bf16[16,112,128]{2,1,0:T(8,128)(2,1)} %bitcast.58), calls=%async_computation.2 | async-start | bytes 917504 | tf_op jit(solution)/shard_map/all_to_all | solution.py:134
  264.8 15.7 %all-to-all-done.2 = bf16[16,112,128]{2,1,0:T(8,128)(2,1)S(1)} async-done(((bf16[16,112,128]{2,1,0:T(8,128)(2,1)}), bf16[16,112,128]{2,1,0:T(8,128)(2,1)S(1)}, u32[]{:S(2)}, u32[]{:S(2)}) %all-to-all-start.2) | async-done | bytes 458784 | tf_op jit(solution)/shard_map/all_to_all | solution.py:134
  (102 shorter events, 9.6 us)
Async XLA Ops:
  6.5 47.5 %copy-start = (bf16[1,112,1792]{2,1,0:T(8,128)(2,1)S(1)}, bf16[1,112,1792]{2,1,0:T(8,128)(2,1)}, u32[]{:S(2)}) copy-start(bf16[1,112,1792]{2,1,0:T(8,128)(2,1)} %param.8) | copy-start | bytes 1204228
  6.5 48.5 %copy-start.2 = (bf16[1,4,112,512]{3,2,1,0:T(8,128)(2,1)S(1)}, bf16[1,4,112,512]{3,2,1,0:T(8,128)(2,1)}, u32[]{:S(2)}) copy-start(bf16[1,4,112,512]{3,2,1,0:T(8,128)(2,1)} %param.10) | copy-start | bytes 1376260
  6.5 54.5 %copy-start.12 = (s32[1,2,4,512]{3,2,1,0:T(4,128)S(1)}, s32[1,2,4,512]{3,2,1,0:T(4,128)}, u32[]{:S(2)}) copy-start(s32[1,2,4,512]{3,2,1,0:T(4,128)} %param.13) | copy-start | bytes 49156
  6.5 93.4 %all-gather.5.cloned.1.call-start = ((), (), s32[]{:S(2)}) async-start(), calls=%async_computation.4 | async-start | bytes 6823936 | tf_op jit(solution)/shard_map/all_gather | solution.py:45
  7.3 124.1 %all-gather.7.cloned.1.call-start = ((), (), s32[]{:S(2)}) async-start(), calls=%async_computation.5 | async-start | bytes 5849088 | tf_op jit(solution)/shard_map/all_gather | solution.py:46
  11.0 42.7 %all-to-all-start = ((bf16[16,2,112,128]{3,2,1,0:T(8,128)(2,1)}), bf16[16,2,112,128]{3,2,1,0:T(8,128)(2,1)S(1)}, u32[]{:S(2)}, u32[]{:S(2)}) async-start(bf16[16,2,112,128]{3,2,1,0:T(8,128)(2,1)} %stack.49), calls=%async_computation | async-start | bytes 1835008 | tf_op jit(solution)/shard_map/all_to_all | solution.py:52
  22.1 45.7 %copy-start.13 = (f32[112]{0:T(128)}, f32[112]{0:T(128)S(1)}, u32[]{:S(2)}) copy-start(f32[112]{0:T(128)S(1)} %compare_convert_fusion) | copy-start | bytes 1348
  54.3 0.6 copy-start.10
  56.6 26.8 %all-to-all-start.1 = ((bf16[16,8,2048]{2,1,0:T(8,128)(2,1)}), bf16[16,8,2048]{2,1,0:T(8,128)(2,1)S(1)}, u32[]{:S(2)}, u32[]{:S(2)}) async-start(bf16[16,8,2048]{2,1,0:T(8,128)(2,1)} %pad_maximum_fusion), calls=%async_computation.1 | async-start | bytes 1048576 | tf_op jit(solution)/shard_map/all_to_all | solution.py:60
  90.8 9.1 %collective-permute-start = (f32[4,8,1792]{2,1,0:T(8,128)S(1)}, f32[4,8,1792]{2,1,0:T(8,128)S(1)}, u32[]{:S(2)}, u32[]{:S(2)}) collective-permute-start(f32[4,8,1792]{2,1,0:T(8,128)S(1)} %pad_maximum_fusion.1), channel_id=1, source_target_pairs={{0,16},{32,48},{64,80},{96,112},{128,144},{160,176},{192,208},{224... | collective-permute-start | bytes 688136 | tf_op jit(solution)/shard_map/ppermute | solution.py:78
  92.5 7.5 %copy-start.6 = (bf16[1792,8]{0,1:T(8,128)(2,1)}, bf16[1792,8]{0,1:T(8,128)(2,1)S(1)}, u32[]{:S(2)}) copy-start(bf16[1792,8]{0,1:T(8,128)(2,1)S(1)} %copy.25) | copy-start | bytes 86020
  99.9 0.7 copy-start.4
  105.8 42.2 %slice-start = ((s8[6422528]{0:T(1024)(128)(4,1)}), s8[2228224]{0:T(1024)(128)(4,1)S(1)}, s32[]{:S(2)}) async-start(s8[6422528]{0:T(1024)(128)(4,1)} %bitcast.316), calls=%async_computation.6 | async-start | bytes 4456448
  131.3 6.4 %copy-start.1 = (bf16[1,3,1792,512]{3,2,1,0:T(8,128)(2,1)S(1)}, bf16[1,3,1792,512]{3,2,1,0:T(8,128)(2,1)}, u32[]{:S(2)}) copy-start(bf16[1,3,1792,512]{3,2,1,0:T(8,128)(2,1)} %all-gather.7.cloned.1.call-done) | copy-start | bytes 16515076
  131.3 9.3 %copy-start.5 = (f32[4,8,1792]{2,1,0:T(8,128)S(1)}, f32[4,8,1792]{2,1,0:T(8,128)}, u32[]{:S(2)}) copy-start(f32[4,8,1792]{2,1,0:T(8,128)} %copy-done.4) | copy-start | bytes 688132
  131.3 16.6 %copy-start.7 = (bf16[1792,8]{0,1:T(8,128)(2,1)S(1)}, bf16[1792,8]{0,1:T(8,128)(2,1)}, u32[]{:S(2)}) copy-start(bf16[1792,8]{0,1:T(8,128)(2,1)} %copy-done.6) | copy-start | bytes 86020
  135.8 12.2 %slice-start.1 = ((s8[6422528]{0:T(1024)(128)(4,1)}), s8[4194304]{0:T(1024)(128)(4,1)S(1)}, s32[]{:S(2)}) async-start(s8[6422528]{0:T(1024)(128)(4,1)} %bitcast.316), calls=%async_computation.7 | async-start | bytes 8388608
  140.7 3.8 %collective-permute-start.1 = (f32[3,8,1792]{2,1,0:T(8,128)S(1)}, f32[3,8,1792]{2,1,0:T(8,128)S(1)}, u32[]{:S(2)}, u32[]{:S(2)}) collective-permute-start(f32[3,8,1792]{2,1,0:T(8,128)S(1)} %slice_add_fusion), channel_id=1, source_target_pairs={{16,32},{80,96},{144,160},{208,224},{17,33},{81,97},{145,161},{209... | collective-permute-start | bytes 516104 | tf_op jit(solution)/shard_map/ppermute | solution.py:83
  141.4 6.5 %collective-permute-start.2 = (f32[3,8,1792]{2,1,0:T(8,128)S(1)}, f32[3,8,1792]{2,1,0:T(8,128)S(1)}, u32[]{:S(2)}, u32[]{:S(2)}) collective-permute-start(f32[3,8,1792]{2,1,0:T(8,128)S(1)} %slice_add_fusion), channel_id=1, source_target_pairs={{48,32},{112,96},{176,160},{240,224},{49,33},{113,97},{177,161},{2... | collective-permute-start | bytes 516104 | tf_op jit(solution)/shard_map/ppermute | solution.py:83
  149.8 6.3 %copy-start.8 = (bf16[8,1792]{1,0:T(8,128)(2,1)}, bf16[8,1792]{1,0:T(8,128)(2,1)S(1)}, u32[]{:S(2)}) copy-start(bf16[8,1792]{1,0:T(8,128)(2,1)S(1)} %fusion.74) | copy-start | bytes 86020
  152.9 1.3 collective-permute-start.3
  153.6 0.7 collective-permute-start.4
  156.1 0.9 copy-start.9
  157.0 1.6 collective-permute-start.5
  157.7 0.9 collective-permute-start.6
  167.0 1.3 collective-permute-start.7
  167.7 0.7 collective-permute-start.8
  174.0 1.3 collective-permute-start.10
  174.6 0.7 collective-permute-start.9
  184.9 2.0 collective-permute-start.11
  185.6 21.5 %collective-permute-start.12 = (bf16[3,8,1792]{2,1,0:T(8,128)(2,1)S(1)}, bf16[3,8,1792]{2,1,0:T(8,128)(2,1)S(1)}, u32[]{:S(2)}, u32[]{:S(2)}) collective-permute-start(bf16[3,8,1792]{2,1,0:T(8,128)(2,1)S(1)} %pad_maximum_fusion.3), channel_id=1, source_target_pairs={{32,48},{96,112},{160,176},{224,240},{33,49},{97,113},{161,177},{2... | collective-permute-start | bytes 258056 | tf_op jit(solution)/shard_map/ppermute | solution.py:119
  219.9 38.0 %copy-start.3 = (bf16[1,4,112,512]{3,2,1,0:T(8,128)(2,1)S(1)}, bf16[1,4,112,512]{3,2,1,0:T(8,128)(2,1)}, u32[]{:S(2)}) copy-start(bf16[1,4,112,512]{3,2,1,0:T(8,128)(2,1)} %param.10) | copy-start | bytes 1376260
  219.9 11.8 %collective-permute-start.13 = (bf16[4,8,1792]{2,1,0:T(8,128)(2,1)S(1)}, bf16[4,8,1792]{2,1,0:T(8,128)(2,1)S(1)}, u32[]{:S(2)}, u32[]{:S(2)}) collective-permute-start(bf16[4,8,1792]{2,1,0:T(8,128)(2,1)S(1)} %pad_maximum_fusion.2), channel_id=1, source_target_pairs={{16,0},{48,32},{80,64},{112,96},{144,128},{176,160},{208,192},{240... | collective-permute-start | bytes 344072 | tf_op jit(solution)/shard_map/ppermute | solution.py:114
  221.7 36.7 %copy-start.11 = (bf16[128,112]{0,1:T(8,128)(2,1)S(1)}, bf16[128,112]{0,1:T(8,128)(2,1)}, u32[]{:S(2)}) copy-start(bf16[128,112]{0,1:T(8,128)(2,1)} %copy-done.10) | copy-start | bytes 86020
  221.7 36.7 %copy-start.14 = (f32[112]{0:T(128)S(1)}, f32[112]{0:T(128)}, u32[]{:S(2)}) copy-start(f32[112]{0:T(128)} %copy-done.13) | copy-start | bytes 1348
  222.3 37.6 %all-to-all-start.3 = ((bf16[16,8,112]{2,1,0:T(8,128)(2,1)}), bf16[16,8,112]{2,1,0:T(8,128)(2,1)S(1)}, u32[]{:S(2)}, u32[]{:S(2)}) async-start(bf16[16,8,112]{2,1,0:T(8,128)(2,1)} %bitcast.315), calls=%async_computation.3 | async-start | bytes 65536 | tf_op jit(solution)/shard_map/all_to_all | solution.py:137
  259.9 20.6 %all-to-all-start.2 = ((bf16[16,112,128]{2,1,0:T(8,128)(2,1)}), bf16[16,112,128]{2,1,0:T(8,128)(2,1)S(1)}, u32[]{:S(2)}, u32[]{:S(2)}) async-start(bf16[16,112,128]{2,1,0:T(8,128)(2,1)} %bitcast.58), calls=%async_computation.2 | async-start | bytes 917504 | tf_op jit(solution)/shard_map/all_to_all | solution.py:134
Sparse Core Ops, SparseCore 0:
  9.2 77.6 all-gather.4
  88.7 42.5 all-gather.6
